TPU v7x, 32 devices: a whole 2x2x4 slice. The times are simulated.
32 devices in a mesh: samples: 16 (over z, y, core), feat: 2 (over x).
Axes of the slice: x: 2, y: 2, z: 4, core: 2. Of those that a mesh axis runs over, the one named last changes fastest.
Arguments:
- samples: float32 [4096, 4096], P('samples', 'feat'), may hold values from -12 to 12, as said below
- factor: float32 [4096, 512], P('feat'), may hold values from -6 to 6
Outputs:
- new_factor: float32 [4096, 512], P('feat')
Inputs may be any that keep to these rules, and one draw needn't show every extreme that they name: `samples`: Real-valued data.
All inputs are finite; a program needn't handle non-finite values.
Results may differ from a plain program's by a relative error of at most 0.00007.
Values sent between devices are 32-bit elements; how exact they have to be, the bound alone decides.
No kernel may reach another device: no remote copies, remote signals or barrier semaphores. Data moves between devices by JAX's collectives and lax.ppermute only.
A program may use at most 64 MiB of HBM per device.

v0:
```python
import jax
import jax.numpy as jnp
from jax import lax
from jax.sharding import PartitionSpec as P

D = 4096
R = 512


def per_device(samples, factor):
    high = lax.Precision.HIGHEST
    contract_rows = (((0,), (0,)), ((), ()))
    scaled = factor * (1.0 / jnp.sqrt(jnp.float32(D)))
    local_proj = jnp.dot(samples, scaled, precision=high, preferred_element_type=jnp.float32)
    proj = lax.psum(local_proj, "feat")
    squared = proj * proj
    rows_total = samples.shape[0] * lax.axis_size("samples")
    half_gram = lax.dot_general(
        scaled, scaled, contract_rows, precision=high, preferred_element_type=jnp.float32
    )
    gram = lax.psum(half_gram, "feat")
    squared_gram = gram * gram
    coef = 6.0 / jnp.sqrt(jnp.float32(D))
    local_moment = lax.dot_general(
        samples, squared, contract_rows, precision=high, preferred_element_type=jnp.float32
    )
    moment = lax.psum(local_moment, "samples") / rows_total
    gram_term = jnp.dot(scaled, squared_gram, precision=high, preferred_element_type=jnp.float32)
    grad = coef * (gram_term - moment)
    total = lax.psum(jnp.sum(grad * grad), "feat")
    rms = jnp.sqrt(total / (D * R)) + 1e-06
    return factor - 0.5 * grad / rms


def solution(mesh):
    placed = (P("samples", "feat"), P("feat", None))
    return jax.shard_map(
        per_device, mesh=mesh, in_specs=placed, out_specs=P("feat", None), check_vma=False
    )
```

profile of v0, /device:TPU:0, one launch (start us, length us, event | category | flops | bytes accessed | tf_op | source)
XLA Modules:
  0.0 228.2 jit_solution(14365884169956142107)
XLA Ops:
  6.5 0.0 copy-start
  6.5 0.0 all-reduce.6.cloned.1.call-start
  6.5 0.0 copy-start.1
  6.5 11.3 %fusion.4 = f32[512,512]{1,0:T(8,128)} fusion(f32[2048,512]{1,0:T(8,128)} %param.3), kind=kOutput, calls=%fused_computation.7 | convolution fusion | flops 6443499520 | bytes 5242880 | tf_op jit(solution)/shard_map/dot_general | solution.py:18
  17.8 0.0 copy-done
  17.8 0.0 copy-done.1
  17.9 7.5 %fusion.11 = f32[256,512]{0,1:T(8,128)} fusion(f32[256,2048]{1,0:T(8,128)S(1)} %copy-done, f32[2048,512]{1,0:T(8,128)S(1)} %copy-done.1), kind=kOutput, calls=%fused_computation.13 | convolution fusion | flops 3222274048 | bytes 6815744 | tf_op jit(solution)/shard_map/dot_general | solution.py:14
  25.4 0.0 all-reduce.6.cloned.1.call-update
  25.4 0.2 all-reduce.4.cloned.1.call-start
  25.6 54.2 %all-reduce.6.cloned.1.call-done = (f32[256,512]{0,1:T(8,128)}, f32[512,512]{1,0:T(8,128)}) async-done(((f32[256,512]{0,1:T(8,128)}, f32[512,512]{1,0:T(8,128)}), (f32[256,512]{0,1:T(8,128)}, f32[512,512]{1,0:T(8,128)})) %all-reduce.6.cloned.1.call-update) | async-done | bytes 1572880 | tf_op jit(solution)/shard_map/psum | solution.py:15
  79.8 6.1 %convolution_bitcast_fusion = f32[2048,512]{1,0:T(8,128)} fusion(f32[256,2048]{1,0:T(8,128)S(1)} %copy-done, f32[256,512]{0,1:T(8,128)} %get-tuple-element.5), kind=kOutput, calls=%fused_computation.9 | convolution fusion | flops 3221356544 | bytes 6815744 | tf_op jit(solution)/shard_map/dot_general | solution.py:24
  86.0 0.0 copy-start.2
  86.0 0.0 all-reduce.4.cloned.1.call-update
  86.0 111.2 %all-reduce.4.cloned.1.call-done = f32[2048,512]{1,0:T(8,128)} async-done(((f32[2048,512]{1,0:T(8,128)}), f32[2048,512]{1,0:T(8,128)}) %all-reduce.4.cloned.1.call-update) | async-done | bytes 4194320 | tf_op jit(solution)/shard_map/psum | solution.py:27
  197.2 0.0 copy-done.2
  197.2 11.5 %multiply_reduce_fusion = (f32[]{:T(128)}, f32[2048,512]{1,0:T(8,128)}) fusion(f32[2048,512]{1,0:T(8,128)} %all-reduce.4.cloned.1.call-done, f32[512,512]{1,0:T(8,128)S(1)} %copy-done.2, f32[2048,512]{1,0:T(8,128)} %param.3), kind=kOutput, calls=%fused_computation.1 | convolution fusion | flops 6449004544 | bytes 13631492 | tf_op jit(solution)/shard_map/dot_general | solution.py:28
  208.7 5.5 %psum.31 = f32[]{:T(128)} all-reduce(f32[]{:T(128)} %get-tuple-element.7), channel_id=1, replica_groups=mesh['samples'=16,'feat'=2] {'feat'}, use_global_device_ids=true, to_apply=%region_4.0 | all-reduce | flops 1 | bytes 8 | tf_op jit(solution)/shard_map/psum | solution.py:30
  214.9 6.5 %divide_subtract_fusion = f32[2048,512]{1,0:T(8,128)} fusion(f32[2048,512]{1,0:T(8,128)} %param.3, f32[2048,512]{1,0:T(8,128)} %get-tuple-element.8, f32[]{:T(128)S(6)} %add.11), kind=kLoop, calls=%fused_computation | loop fusion | flops 3145728 | bytes 12582916 | tf_op jit(solution)/shard_map/sub | solution.py:32
Async XLA Ops:
  6.5 11.3 %copy-start = (f32[256,2048]{1,0:T(8,128)S(1)}, f32[256,2048]{1,0:T(8,128)}, u32[]{:S(2)}) copy-start(f32[256,2048]{1,0:T(8,128)} %param.2) | copy-start | bytes 6291460
  6.5 73.3 %all-reduce.6.cloned.1.call-start = ((), (), s32[]{:S(2)}) async-start(), calls=%async_computation.1 | async-start | bytes 3145728 | tf_op jit(solution)/shard_map/psum | solution.py:15
  6.5 11.3 %copy-start.1 = (f32[2048,512]{1,0:T(8,128)S(1)}, f32[2048,512]{1,0:T(8,128)}, u32[]{:S(2)}) copy-start(f32[2048,512]{1,0:T(8,128)} %param.3) | copy-start | bytes 12582916
  25.4 171.8 %all-reduce.4.cloned.1.call-start = ((), (), s32[]{:S(2)}) async-start(), calls=%async_computation | async-start | bytes 8388608 | tf_op jit(solution)/shard_map/psum | solution.py:27
  86.0 111.2 %copy-start.2 = (f32[512,512]{1,0:T(8,128)S(1)}, f32[512,512]{1,0:T(8,128)}, u32[]{:S(2)}) copy-start(f32[512,512]{1,0:T(8,128)} %get-tuple-element.6) | copy-start | bytes 3145732
Sparse Core Ops, SparseCore 0:
  25.5 54.2 all-reduce.5
  86.1 111.0 all-reduce.3
where the time goes:
time: 228 us
  waiting for transfers between devices  165 us (72%)
  matrix products  36.5 us (16%)
  between operations  14 us (6%)
  other arithmetic  6.53 us (3%)
  blocking collectives  5.53 us (2%)
    psum x1, waiting for transfers between devices, per_device(): moment = lax.psum(local_moment, 'samples') / rows_total  111 us
    psum x1, waiting for transfers between devices, per_device(): proj = lax.psum(local_proj, 'feat')  54.2 us
    dot_general x1, matrix products, per_device(): jnp.dot(scaled, squared_gram, precision=high, preferred_element_type=jnp....  11.5 us
    dot_general x1, matrix products, per_device(): lax.dot_general(scaled, scaled, contract_rows, precision=high, preferred_...  11.3 us
    dot_general x1, matrix products, per_device(): jnp.dot(samples, scaled, precision=high, preferred_element_type=jnp.float32)  7.54 us
    sub x1, other arithmetic, per_device(): return factor - 0.5 * grad / rms  6.53 us
    dot_general x1, matrix products, per_device(): lax.dot_general(samples, squared, contract_rows, precision=high, preferre...  6.14 us
    psum x1, blocking collectives, per_device(): total = lax.psum(jnp.sum(grad * grad), 'feat')  5.53 us
  transfers between devices with their start and end apart: 2, of which 2 were waited for; matrix products, arithmetic and copies ran while one was open for 0% of the time, Pallas kernels for 0%

commit v1 on v0

--- a/solution.py
+++ b/solution.py
@@ -12,7 +12,7 @@
     contract_rows = (((0,), (0,)), ((), ()))
     scaled = factor * (1.0 / jnp.sqrt(jnp.float32(D)))
     local_proj = jnp.dot(samples, scaled, precision=high, preferred_element_type=jnp.float32)
-    proj = lax.psum(local_proj, "feat")
+    proj = local_proj + lax.ppermute(local_proj, "feat", [(0, 1), (1, 0)])
     squared = proj * proj
     rows_total = samples.shape[0] * lax.axis_size("samples")
     half_gram = lax.dot_general(

time: 228 us -> 217 us (0.952)
  waiting for transfers between devices: 165 us -> 149 us
  starting transfers between devices: 0.22 us -> 3.26 us
    psum x1, waiting for transfers between devices: 54.2 us -> 13.2 us  [per_device(): gram = lax.psum(half_gram, 'feat')]
    ppermute x0 -> x1, waiting for transfers between devices: none -> 20.7 us  [per_device(): proj = local_proj + lax.ppermute(local_proj, 'feat', [(0, 1), (1, 0)])]
    psum x1, waiting for transfers between devices: 111 us -> 115 us  [per_device(): moment = lax.psum(local_moment, 'samples') / rows_total]
    ppermute x0 -> x1, starting transfers between devices: none -> 3.04 us  [per_device(): proj = local_proj + lax.ppermute(local_proj, 'feat', [(0, 1), (1, 0)])]
  transfers between devices with their start and end apart: 2 -> 3, of which waited for: 2 -> 3; matrix products, arithmetic and copies ran while one was open for 0% -> 6% of each run, Pallas kernels for 0% -> 0%
where the time goes in v1:
time: 217 us
  waiting for transfers between devices  149 us (69%)
  matrix products  37 us (17%)
  between operations  14.1 us (6%)
  other arithmetic  8.26 us (4%)
  blocking collectives  5.55 us (3%)
  starting transfers between devices  3.26 us (2%)
    psum x1, waiting for transfers between devices, per_device(): moment = lax.psum(local_moment, 'samples') / rows_total  115 us
    ppermute x1, waiting for transfers between devices, per_device(): proj = local_proj + lax.ppermute(local_proj, 'feat', [(0, 1), (1, 0)])  20.7 us
    psum x1, waiting for transfers between devices, per_device(): gram = lax.psum(half_gram, 'feat')  13.2 us
    dot_general x1, matrix products, per_device(): jnp.dot(scaled, squared_gram, precision=high, preferred_element_type=jnp....  11.8 us
    dot_general x1, matrix products, per_device(): lax.dot_general(scaled, scaled, contract_rows, precision=high, preferred_...  11.3 us
    dot_general x1, matrix products, per_device(): jnp.dot(samples, scaled, precision=high, preferred_element_type=jnp.float32)  8.7 us
    sub x1, other arithmetic, per_device(): return factor - 0.5 * grad / rms  8.26 us
    psum x1, blocking collectives, per_device(): total = lax.psum(jnp.sum(grad * grad), 'feat')  5.55 us
  transfers between devices with their start and end apart: 3, of which 3 were waited for; matrix products, arithmetic and copies ran while one was open for 6% of the time, Pallas kernels for 0%

profile of v1, /device:TPU:0, one launch (start us, length us, event | category | flops | bytes accessed | tf_op | source)
XLA Modules:
  0.0 216.8 jit_solution(13439632795177544095)
XLA Ops:
  6.5 0.0 copy-start
  6.5 0.0 all-reduce.3.cloned.1.call-start
  6.5 11.3 %fusion.4 = f32[512,512]{1,0:T(8,128)} fusion(f32[2048,512]{1,0:T(8,128)} %param.3), kind=kOutput, calls=%fused_computation.7 | convolution fusion | flops 6443499520 | bytes 5242880 | tf_op jit(solution)/shard_map/dot_general | solution.py:18
  17.9 0.0 all-reduce.3.cloned.1.call-update
  17.9 0.2 all-reduce.5.cloned.1.call-start
  18.1 0.0 copy-done
  18.1 8.7 %fusion.9 = f32[256,512]{0,1:T(8,128)S(1)} fusion(f32[256,2048]{1,0:T(8,128)S(1)} %copy-done, f32[2048,512]{1,0:T(8,128)} %param.3), kind=kOutput, calls=%fused_computation.13 | convolution fusion | flops 3222274048 | bytes 6815744 | tf_op jit(solution)/shard_map/dot_general | solution.py:14
  26.9 3.0 %collective-permute-start = (f32[256,512]{0,1:T(8,128)S(1)}, f32[256,512]{0,1:T(8,128)S(1)}, u32[]{:S(2)}, u32[]{:S(2)}) collective-permute-start(f32[256,512]{0,1:T(8,128)S(1)} %fusion.9), channel_id=1, source_target_pairs={{0,1},{1,0},{2,3},{3,2},{4,5},{5,4},{6,7},{7,6},{8,9},{9,8},{10,11... | collective-permute-start | bytes 1572872 | tf_op jit(solution)/shard_map/ppermute | solution.py:15
  29.9 20.7 %collective-permute-done = f32[256,512]{0,1:T(8,128)S(1)} collective-permute-done((f32[256,512]{0,1:T(8,128)S(1)}, f32[256,512]{0,1:T(8,128)S(1)}, u32[]{:S(2)}, u32[]{:S(2)}) %collective-permute-start) | collective-permute-done | bytes 524320 | tf_op jit(solution)/shard_map/ppermute | solution.py:15
  50.6 5.2 %convolution_bitcast_fusion = f32[2048,512]{1,0:T(8,128)} fusion(f32[256,2048]{1,0:T(8,128)S(1)} %copy-done, f32[256,512]{0,1:T(8,128)S(1)} %fusion.9, f32[256,512]{0,1:T(8,128)S(1)} %collective-permute-done), kind=kOutput, calls=%fused_computation.9 | convolution fusion | flops 3221487616 | bytes 7340032 | tf_op jit(solution)/shard_map/dot_general | solution.py:24
  55.8 0.0 all-reduce.5.cloned.1.call-update
  55.8 13.2 %all-reduce.3.cloned.1.call-done = f32[512,512]{1,0:T(8,128)} async-done(((f32[512,512]{1,0:T(8,128)}), f32[512,512]{1,0:T(8,128)}) %all-reduce.3.cloned.1.call-update) | async-done | bytes 1048592 | tf_op jit(solution)/shard_map/psum | solution.py:21
  69.0 114.7 %all-reduce.5.cloned.1.call-done = f32[2048,512]{1,0:T(8,128)} async-done(((f32[2048,512]{1,0:T(8,128)}), f32[2048,512]{1,0:T(8,128)}) %all-reduce.5.cloned.1.call-update) | async-done | bytes 4194320 | tf_op jit(solution)/shard_map/psum | solution.py:27
  183.7 11.8 %multiply_reduce_fusion = (f32[]{:T(128)}, f32[2048,512]{1,0:T(8,128)}) fusion(f32[2048,512]{1,0:T(8,128)} %all-reduce.5.cloned.1.call-done, f32[512,512]{1,0:T(8,128)} %all-reduce.3.cloned.1.call-done, f32[2048,512]{1,0:T(8,128)} %param.3), kind=kOutput, calls=%fused_computation.1 | convolution fusion | flops 6449004544 | bytes 13631492 | tf_op jit(solution)/shard_map/dot_general | solution.py:28
  195.5 5.5 %psum.23 = f32[]{:T(128)} all-reduce(f32[]{:T(128)} %get-tuple-element.5), channel_id=1, replica_groups=mesh['samples'=16,'feat'=2] {'feat'}, use_global_device_ids=true, to_apply=%region_3.0 | all-reduce | flops 1 | bytes 8 | tf_op jit(solution)/shard_map/psum | solution.py:30
  201.7 8.3 %divide_subtract_fusion = f32[2048,512]{1,0:T(8,128)} fusion(f32[2048,512]{1,0:T(8,128)} %param.3, f32[]{:T(128)S(6)} %add.13, f32[2048,512]{1,0:T(8,128)} %get-tuple-element.6, f32[2048,512]{1,0:T(8,128)} %all-reduce.5.cloned.1.call-done), kind=kLoop, calls=%fused_computation | loop fusion | flops 5242880 | bytes 16777220 | tf_op jit(solution)/shard_map/sub | solution.py:32
Async XLA Ops:
  6.5 11.6 %copy-start = (f32[256,2048]{1,0:T(8,128)S(1)}, f32[256,2048]{1,0:T(8,128)}, u32[]{:S(2)}) copy-start(f32[256,2048]{1,0:T(8,128)} %param.2) | copy-start | bytes 6291460
  6.5 62.5 %all-reduce.3.cloned.1.call-start = ((), (), s32[]{:S(2)}) async-start(), calls=%async_computation | async-start | bytes 2097152 | tf_op jit(solution)/shard_map/psum | solution.py:21
  17.9 165.8 %all-reduce.5.cloned.1.call-start = ((), (), s32[]{:S(2)}) async-start(), calls=%async_computation.1 | async-start | bytes 8388608 | tf_op jit(solution)/shard_map/psum | solution.py:27
  26.9 23.7 %collective-permute-start = (f32[256,512]{0,1:T(8,128)S(1)}, f32[256,512]{0,1:T(8,128)S(1)}, u32[]{:S(2)}, u32[]{:S(2)}) collective-permute-start(f32[256,512]{0,1:T(8,128)S(1)} %fusion.9), channel_id=1, source_target_pairs={{0,1},{1,0},{2,3},{3,2},{4,5},{5,4},{6,7},{7,6},{8,9},{9,8},{10,11... | collective-permute-start | bytes 1572872 | tf_op jit(solution)/shard_map/ppermute | solution.py:15
Sparse Core Ops, SparseCore 0:
  18.0 50.9 all-reduce.2
  72.7 110.9 all-reduce.4
